TPU v7x, 512 devices: a whole 4x4x16 slice. The times are simulated.
512 devices in a mesh: ctx: 64 (over y, z), head: 8 (over x, core).
Axes of the slice: x: 4, y: 4, z: 16, core: 2. Of those that a mesh axis runs over, the one named last changes fastest.
Arguments:
- queries: bfloat16 [32768, 4096], P(('ctx', 'head')), may hold values from -12 to 12
- keys: bfloat16 [32768, 1024], P(('ctx', 'head')), may hold values from -12 to 12
- values: bfloat16 [32768, 1024], P(('ctx', 'head')), may hold values from -6 to 6
- doc_lengths: int32 [16], replicated, may hold values from 1 to 4096, 32768 in all
- piece_owner: int32 [64, 64], P('ctx'), may hold values from 0 to 63, each once within a row
Outputs:
- owned: bfloat16 [32768, 4096], P('ctx', 'head')
Inputs may be any that keep to these rules, and one draw needn't show every extreme that they name: Each row of piece_owner is a permutation of 0 .. 63. doc_lengths sum to 32768, and the largest equals 4096.
All inputs are finite; a program needn't handle non-finite values.
Results may differ from a plain program's by a relative error of at most 0.0033.
Values may be sent and summed in bfloat16 or wider, within the bound.
A program may use at most 64 MiB of HBM per device.

v0:
```python
import math

import jax
import jax.numpy as jnp
from jax import lax
from jax.sharding import PartitionSpec as P

HD = 128
QPK = 4
MOST = 4096


masked_score = -1e30


def passed_along(value, axis, steps):
    count = lax.axis_size(axis)
    leading, last = (max(0, -steps), min(count, count - steps))
    return lax.ppermute(value, axis, [(source, source + steps) for source in range(leading, last)])


def doc_index(positions, doc_lengths):
    doc_ends = jnp.cumsum(doc_lengths)
    return jnp.sum((positions[:, None] >= doc_ends[None, :]).astype(jnp.int32), axis=1)


def per_device(queries, keys, values, doc_lengths, piece_owner):
    query_rows, key_rows, value_rows = (
        lax.all_to_all(queries, "head", split_axis=1, concat_axis=0, tiled=True),
        lax.all_to_all(keys, "head", split_axis=1, concat_axis=0, tiled=True),
        lax.all_to_all(values, "head", split_axis=1, concat_axis=0, tiled=True),
    )
    tokens_here = query_rows.shape[0]
    groups = key_rows.shape[1] // HD
    features = query_rows.shape[1]
    reach_back = (MOST - 1) // tokens_here + 1
    score_scale = 1.0 / math.sqrt(HD)
    ctx_place = lax.axis_index("ctx")
    offsets = jnp.arange(tokens_here, dtype=jnp.int32)
    query_position = ctx_place * tokens_here + offsets
    query_ids = doc_index(query_position, doc_lengths)
    paired = jnp.stack([key_rows, value_rows])
    shards = [paired]
    for distance in range(1, reach_back + 1):
        shards.append(passed_along(paired, "ctx", distance))
    key_positions = []
    key_ids = []
    for distance in range(reach_back + 1):
        shard_position = (ctx_place - distance) * tokens_here + offsets
        key_positions.append(shard_position)
        key_ids.append(doc_index(shard_position, doc_lengths))
    block_rows = 512
    block_count = tokens_here // block_rows
    query_split = query_rows.reshape(block_count, block_rows, groups, QPK, HD)
    position_split = query_position.reshape(block_count, block_rows)
    ids_split = query_ids.reshape(block_count, block_rows)

    def attend(operands):
        query_block, position_block, ids_block = operands
        row_top = jnp.full((block_rows, groups, QPK), masked_score, jnp.float32)
        row_total = jnp.zeros((block_rows, groups, QPK), jnp.float32)
        weighted = jnp.zeros((block_rows, groups, QPK, HD), jnp.float32)
        carry_state = (row_top, row_total, weighted)
        for distance in range(reach_back + 1):
            shard_pair = shards[distance]
            shard_keys = shard_pair[0].reshape(tokens_here, groups, HD)
            shard_values = shard_pair[1].reshape(tokens_here, groups, HD)
            live_pairs = (
                (key_positions[distance][None, :] >= 0)
                & (key_positions[distance][None, :] <= position_block[:, None])
                & (key_ids[distance][None, :] == ids_block[:, None])
            )

            def update(
                state_now, shard_keys=shard_keys, shard_values=shard_values, live_pairs=live_pairs
            ):
                old_top, old_total, old_weighted = state_now
                live_mask = live_pairs[:, None, None, :]
                scores = (
                    jnp.einsum(
                        "qgjd,kgd->qgjk",
                        query_block,
                        shard_keys,
                        preferred_element_type=jnp.float32,
                    )
                    * score_scale
                )
                scores = jnp.where(live_mask, scores, masked_score)
                new_top = jnp.maximum(old_top, jnp.max(scores, axis=-1))
                factor = jnp.exp(old_top - new_top)
                weights = jnp.where(live_mask, jnp.exp(scores - new_top[..., None]), 0.0)
                new_total = old_total * factor + jnp.sum(weights, axis=-1)
                new_weighted = old_weighted * factor[..., None] + jnp.einsum(
                    "qgjk,kgd->qgjd",
                    weights.astype(jnp.bfloat16),
                    shard_values,
                    preferred_element_type=jnp.float32,
                )
                return (new_top, new_total, new_weighted)

            carry_state = update(carry_state)
        final_top, final_total, final_weighted = carry_state
        result = final_weighted / final_total[..., None]
        return result.astype(jnp.bfloat16).reshape(block_rows, groups * QPK * HD)

    attended = lax.map(attend, (query_split, position_split, ids_split)).reshape(
        tokens_here, features
    )
    ctx_count = lax.axis_size("ctx")
    piece_rows = tokens_here // ctx_count
    owner_row = piece_owner[0]
    slot_index = jnp.arange(ctx_count, dtype=jnp.int32)
    matches = owner_row[:, None] == slot_index[None, :]
    inverse = jnp.sum(jnp.where(matches, slot_index[:, None], 0), axis=0)
    pieces = attended.reshape(ctx_count, piece_rows, features)
    ordered = jnp.take(pieces, inverse, axis=0)
    received = lax.all_to_all(ordered, "ctx", split_axis=0, concat_axis=0, tiled=True)
    return received.reshape(tokens_here, features)


def solution(mesh):
    return jax.shard_map(
        per_device,
        mesh=mesh,
        in_specs=(
            P(("ctx", "head"), None),
            P(("ctx", "head"), None),
            P(("ctx", "head"), None),
            P(),
            P("ctx", None),
        ),
        out_specs=P("ctx", "head"),
        check_vma=False,
    )
```

profile of v0, /device:TPU:1, one launch (start us, length us, event | category | flops | bytes accessed | tf_op | source)
XLA Modules:
  0.0 321.9 jit_solution(12941780340591550754)
XLA Ops:
  0.0 0.9 copy-done
  1.6 10.1 %all-to-all-start = ((bf16[64,8,128]{2,0,1:T(8,128)(2,1)}), bf16[64,8,128]{2,0,1:T(8,128)(2,1)S(1)}, u32[]{:S(2)}, u32[]{:S(2)}) async-start(bf16[64,8,128]{2,0,1:T(8,128)(2,1)} %copy_bitcast_fusion.2), calls=%async_computation | async-start | bytes 262144 | tf_op jit(solution)/shard_map/all_to_all | solution.py:30
  13.5 1.6 copy_bitcast_fusion.1
  15.2 2.7 compare_and_fusion.8
  17.9 4.8 %all-to-all-start.2 = ((bf16[64,8,128]{2,0,1:T(8,128)(2,1)}), bf16[64,8,128]{2,0,1:T(8,128)(2,1)S(1)}, u32[]{:S(2)}, u32[]{:S(2)}) async-start(bf16[64,8,128]{2,0,1:T(8,128)(2,1)} %copy_bitcast_fusion.1), calls=%async_computation.2 | async-start | bytes 262144 | tf_op jit(solution)/shard_map/all_to_all | solution.py:31
  22.8 1.9 copy.187
  24.6 3.3 %all-to-all-done.2 = bf16[64,8,128]{2,0,1:T(8,128)(2,1)S(1)} async-done(((bf16[64,8,128]{2,0,1:T(8,128)(2,1)}), bf16[64,8,128]{2,0,1:T(8,128)(2,1)S(1)}, u32[]{:S(2)}, u32[]{:S(2)}) %all-to-all-start.2) | async-done | bytes 131104 | tf_op jit(solution)/shard_map/all_to_all | solution.py:31
  28.0 4.3 %all-to-all-start.1 = ((bf16[64,8,512]{2,0,1:T(8,128)(2,1)}), bf16[64,8,512]{2,0,1:T(8,128)(2,1)S(1)}, u32[]{:S(2)}, u32[]{:S(2)}) async-start(bf16[64,8,512]{2,0,1:T(8,128)(2,1)} %bitcast.463), calls=%async_computation.1 | async-start | bytes 1048576 | tf_op jit(solution)/shard_map/all_to_all | solution.py:29
  32.3 1.2 compare_and_fusion.7
  34.2 11.8 %collective-permute-start.7 = (bf16[2,512,128]{2,1,0:T(8,128)(2,1)}, bf16[2,512,128]{2,1,0:T(8,128)(2,1)}, u32[]{:S(2)}, u32[]{:S(2)}) collective-permute-start(bf16[2,512,128]{2,1,0:T(8,128)(2,1)} %pad_maximum_fusion), channel_id=1, source_target_pairs={{0,64},{8,72},{16,80},{24,88},{32,96},{40,104},{48,112},{56,120},{... | collective-permute-start | bytes 786440 | tf_op jit(solution)/shard_map/ppermute | solution.py:19
  46.0 6.1 %collective-permute-start.6 = (bf16[2,512,128]{2,1,0:T(8,128)(2,1)}, bf16[2,512,128]{2,1,0:T(8,128)(2,1)}, u32[]{:S(2)}, u32[]{:S(2)}) collective-permute-start(bf16[2,512,128]{2,1,0:T(8,128)(2,1)} %pad_maximum_fusion), channel_id=1, source_target_pairs={{0,56},{8,64},{16,72},{24,80},{32,88},{40,96},{48,104},{56,112},{6... | collective-permute-start | bytes 786440 | tf_op jit(solution)/shard_map/ppermute | solution.py:19
  52.1 4.4 %collective-permute-start.5 = (bf16[2,512,128]{2,1,0:T(8,128)(2,1)}, bf16[2,512,128]{2,1,0:T(8,128)(2,1)}, u32[]{:S(2)}, u32[]{:S(2)}) collective-permute-start(bf16[2,512,128]{2,1,0:T(8,128)(2,1)} %pad_maximum_fusion), channel_id=1, source_target_pairs={{0,48},{8,56},{16,64},{24,72},{32,80},{40,88},{48,96},{56,104},{64... | collective-permute-start | bytes 786440 | tf_op jit(solution)/shard_map/ppermute | solution.py:19
  56.5 8.4 %collective-permute-start.4 = (bf16[2,512,128]{2,1,0:T(8,128)(2,1)}, bf16[2,512,128]{2,1,0:T(8,128)(2,1)}, u32[]{:S(2)}, u32[]{:S(2)}) collective-permute-start(bf16[2,512,128]{2,1,0:T(8,128)(2,1)} %pad_maximum_fusion), channel_id=1, source_target_pairs={{0,40},{8,48},{16,56},{24,64},{32,72},{40,80},{48,88},{56,96},{64,... | collective-permute-start | bytes 786440 | tf_op jit(solution)/shard_map/ppermute | solution.py:19
  64.9 3.1 collective-permute-start.1
  68.1 0.9 fusion
  69.0 110.9 %collective-permute-done.1 = bf16[2,512,128]{2,1,0:T(8,128)(2,1)} collective-permute-done((bf16[2,512,128]{2,1,0:T(8,128)(2,1)}, bf16[2,512,128]{2,1,0:T(8,128)(2,1)}, u32[]{:S(2)}, u32[]{:S(2)}) %collective-permute-start.1) | collective-permute-done | bytes 262176 | tf_op jit(solution)/shard_map/ppermute | solution.py:19
  179.9 5.4 %collective-permute-start.2 = (bf16[2,512,128]{2,1,0:T(8,128)(2,1)}, bf16[2,512,128]{2,1,0:T(8,128)(2,1)S(1)}, u32[]{:S(2)}, u32[]{:S(2)}) collective-permute-start(bf16[2,512,128]{2,1,0:T(8,128)(2,1)} %pad_maximum_fusion), channel_id=1, source_target_pairs={{0,24},{8,32},{16,40},{24,48},{32,56},{40,64},{48,72},{56,80},{64,... | collective-permute-start | bytes 786440 | tf_op jit(solution)/shard_map/ppermute | solution.py:19
  185.3 1.8 fusion.2
  187.1 7.4 %collective-permute-done.2 = bf16[2,512,128]{2,1,0:T(8,128)(2,1)S(1)} collective-permute-done((bf16[2,512,128]{2,1,0:T(8,128)(2,1)}, bf16[2,512,128]{2,1,0:T(8,128)(2,1)S(1)}, u32[]{:S(2)}, u32[]{:S(2)}) %collective-permute-start.2) | collective-permute-done | bytes 262176 | tf_op jit(solution)/shard_map/ppermute | solution.py:19
  194.5 14.2 %collective-permute-start.3 = (bf16[2,512,128]{2,1,0:T(8,128)(2,1)}, bf16[2,512,128]{2,1,0:T(8,128)(2,1)S(1)}, u32[]{:S(2)}, u32[]{:S(2)}) collective-permute-start(bf16[2,512,128]{2,1,0:T(8,128)(2,1)} %pad_maximum_fusion), channel_id=1, source_target_pairs={{0,32},{8,40},{16,48},{24,56},{32,64},{40,72},{48,80},{56,88},{64,... | collective-permute-start | bytes 786440 | tf_op jit(solution)/shard_map/ppermute | solution.py:19
  208.7 0.9 fusion.3
  209.6 13.3 %collective-permute-done.3 = bf16[2,512,128]{2,1,0:T(8,128)(2,1)S(1)} collective-permute-done((bf16[2,512,128]{2,1,0:T(8,128)(2,1)}, bf16[2,512,128]{2,1,0:T(8,128)(2,1)S(1)}, u32[]{:S(2)}, u32[]{:S(2)}) %collective-permute-start.3) | collective-permute-done | bytes 262176 | tf_op jit(solution)/shard_map/ppermute | solution.py:19
  222.9 10.6 %collective-permute-start = (bf16[2,512,128]{2,1,0:T(8,128)(2,1)}, bf16[2,512,128]{2,1,0:T(8,128)(2,1)S(1)}, u32[]{:S(2)}, u32[]{:S(2)}) collective-permute-start(bf16[2,512,128]{2,1,0:T(8,128)(2,1)} %pad_maximum_fusion), channel_id=1, source_target_pairs={{0,8},{8,16},{16,24},{24,32},{32,40},{40,48},{48,56},{56,64},{64,7... | collective-permute-start | bytes 786440 | tf_op jit(solution)/shard_map/ppermute | solution.py:19
  233.5 0.9 fusion.4
  234.5 1.8 fusion.5
  236.3 1.8 fusion.6
  238.8 0.9 fusion.1
  239.7 1.8 fusion.7
  241.5 1.8 fusion.8
  243.4 1.1 fusion.9
  244.4 1.1 fusion.25
  245.5 1.0 fusion.23
  246.5 1.0 fusion.21
  247.6 1.0 fusion.19
  248.6 1.1 fusion.17
  249.7 1.3 fusion.15
  251.0 1.0 fusion.13
  252.0 1.0 fusion.11
  253.1 2.1 fusion.93
  255.2 2.4 fusion.66
  257.6 2.4 fusion.69
  260.0 2.4 fusion.72
  262.4 1.5 fusion.75
  263.9 1.5 fusion.78
  265.4 2.4 fusion.81
  267.9 3.1 fusion.141
  271.0 2.9 divide_convert_fusion
  275.3 45.8 %all_to_all.53 = bf16[64,8,512]{2,1,0:T(8,128)(2,1)S(1)} all-to-all(bf16[64,8,512]{2,1,0:T(8,128)(2,1)S(1)} %broadcast_select_fusion), channel_id=1, replica_groups=mesh['ctx'=64,'head'=8] {'ctx'}, dimensions={0} | all-to-all | bytes 1048576 | tf_op jit(solution)/shard_map/all_to_all | solution.py:117
  (50 shorter events, 6.3 us)
Async XLA Ops:
  0.0 0.9 copy-start
  1.6 16.3 %all-to-all-start = ((bf16[64,8,128]{2,0,1:T(8,128)(2,1)}), bf16[64,8,128]{2,0,1:T(8,128)(2,1)S(1)}, u32[]{:S(2)}, u32[]{:S(2)}) async-start(bf16[64,8,128]{2,0,1:T(8,128)(2,1)} %copy_bitcast_fusion.2), calls=%async_computation | async-start | bytes 262144 | tf_op jit(solution)/shard_map/all_to_all | solution.py:30
  17.9 10.1 %all-to-all-start.2 = ((bf16[64,8,128]{2,0,1:T(8,128)(2,1)}), bf16[64,8,128]{2,0,1:T(8,128)(2,1)S(1)}, u32[]{:S(2)}, u32[]{:S(2)}) async-start(bf16[64,8,128]{2,0,1:T(8,128)(2,1)} %copy_bitcast_fusion.1), calls=%async_computation.2 | async-start | bytes 262144 | tf_op jit(solution)/shard_map/all_to_all | solution.py:31
  28.0 40.0 %all-to-all-start.1 = ((bf16[64,8,512]{2,0,1:T(8,128)(2,1)}), bf16[64,8,512]{2,0,1:T(8,128)(2,1)S(1)}, u32[]{:S(2)}, u32[]{:S(2)}) async-start(bf16[64,8,512]{2,0,1:T(8,128)(2,1)} %bitcast.463), calls=%async_computation.1 | async-start | bytes 1048576 | tf_op jit(solution)/shard_map/all_to_all | solution.py:29
  34.2 207.3 %collective-permute-start.7 = (bf16[2,512,128]{2,1,0:T(8,128)(2,1)}, bf16[2,512,128]{2,1,0:T(8,128)(2,1)}, u32[]{:S(2)}, u32[]{:S(2)}) collective-permute-start(bf16[2,512,128]{2,1,0:T(8,128)(2,1)} %pad_maximum_fusion), channel_id=1, source_target_pairs={{0,64},{8,72},{16,80},{24,88},{32,96},{40,104},{48,112},{56,120},{... | collective-permute-start | bytes 786440 | tf_op jit(solution)/shard_map/ppermute | solution.py:19
  46.0 193.7 %collective-permute-start.6 = (bf16[2,512,128]{2,1,0:T(8,128)(2,1)}, bf16[2,512,128]{2,1,0:T(8,128)(2,1)}, u32[]{:S(2)}, u32[]{:S(2)}) collective-permute-start(bf16[2,512,128]{2,1,0:T(8,128)(2,1)} %pad_maximum_fusion), channel_id=1, source_target_pairs={{0,56},{8,64},{16,72},{24,80},{32,88},{40,96},{48,104},{56,112},{6... | collective-permute-start | bytes 786440 | tf_op jit(solution)/shard_map/ppermute | solution.py:19
  52.1 184.2 %collective-permute-start.5 = (bf16[2,512,128]{2,1,0:T(8,128)(2,1)}, bf16[2,512,128]{2,1,0:T(8,128)(2,1)}, u32[]{:S(2)}, u32[]{:S(2)}) collective-permute-start(bf16[2,512,128]{2,1,0:T(8,128)(2,1)} %pad_maximum_fusion), channel_id=1, source_target_pairs={{0,48},{8,56},{16,64},{24,72},{32,80},{40,88},{48,96},{56,104},{64... | collective-permute-start | bytes 786440 | tf_op jit(solution)/shard_map/ppermute | solution.py:19
  56.5 178.0 %collective-permute-start.4 = (bf16[2,512,128]{2,1,0:T(8,128)(2,1)}, bf16[2,512,128]{2,1,0:T(8,128)(2,1)}, u32[]{:S(2)}, u32[]{:S(2)}) collective-permute-start(bf16[2,512,128]{2,1,0:T(8,128)(2,1)} %pad_maximum_fusion), channel_id=1, source_target_pairs={{0,40},{8,48},{16,56},{24,64},{32,72},{40,80},{48,88},{56,96},{64,... | collective-permute-start | bytes 786440 | tf_op jit(solution)/shard_map/ppermute | solution.py:19
  64.9 115.0 %collective-permute-start.1 = (bf16[2,512,128]{2,1,0:T(8,128)(2,1)}, bf16[2,512,128]{2,1,0:T(8,128)(2,1)}, u32[]{:S(2)}, u32[]{:S(2)}) collective-permute-start(bf16[2,512,128]{2,1,0:T(8,128)(2,1)} %pad_maximum_fusion), channel_id=1, source_target_pairs={{0,16},{8,24},{16,32},{24,40},{32,48},{40,56},{48,64},{56,72},{64,... | collective-permute-start | bytes 786440 | tf_op jit(solution)/shard_map/ppermute | solution.py:19
  179.9 14.6 %collective-permute-start.2 = (bf16[2,512,128]{2,1,0:T(8,128)(2,1)}, bf16[2,512,128]{2,1,0:T(8,128)(2,1)S(1)}, u32[]{:S(2)}, u32[]{:S(2)}) collective-permute-start(bf16[2,512,128]{2,1,0:T(8,128)(2,1)} %pad_maximum_fusion), channel_id=1, source_target_pairs={{0,24},{8,32},{16,40},{24,48},{32,56},{40,64},{48,72},{56,80},{64,... | collective-permute-start | bytes 786440 | tf_op jit(solution)/shard_map/ppermute | solution.py:19
  194.5 40.0 %copy-start.4 = (bf16[2,512,128]{2,1,0:T(8,128)(2,1)}, bf16[2,512,128]{2,1,0:T(8,128)(2,1)S(1)}, u32[]{:S(2)}) copy-start(bf16[2,512,128]{2,1,0:T(8,128)(2,1)S(1)} %collective-permute-done.2) | copy-start | bytes 786436
  194.5 28.5 %collective-permute-start.3 = (bf16[2,512,128]{2,1,0:T(8,128)(2,1)}, bf16[2,512,128]{2,1,0:T(8,128)(2,1)S(1)}, u32[]{:S(2)}, u32[]{:S(2)}) collective-permute-start(bf16[2,512,128]{2,1,0:T(8,128)(2,1)} %pad_maximum_fusion), channel_id=1, source_target_pairs={{0,32},{8,40},{16,48},{24,56},{32,64},{40,72},{48,80},{56,88},{64,... | collective-permute-start | bytes 786440 | tf_op jit(solution)/shard_map/ppermute | solution.py:19
  222.9 13.3 %copy-start.6 = (bf16[2,512,128]{2,1,0:T(8,128)(2,1)}, bf16[2,512,128]{2,1,0:T(8,128)(2,1)S(1)}, u32[]{:S(2)}) copy-start(bf16[2,512,128]{2,1,0:T(8,128)(2,1)S(1)} %collective-permute-done.3) | copy-start | bytes 786436
  222.9 15.8 %collective-permute-start = (bf16[2,512,128]{2,1,0:T(8,128)(2,1)}, bf16[2,512,128]{2,1,0:T(8,128)(2,1)S(1)}, u32[]{:S(2)}, u32[]{:S(2)}) collective-permute-start(bf16[2,512,128]{2,1,0:T(8,128)(2,1)} %pad_maximum_fusion), channel_id=1, source_target_pairs={{0,8},{8,16},{16,24},{24,32},{32,40},{40,48},{48,56},{56,64},{64,7... | collective-permute-start | bytes 786440 | tf_op jit(solution)/shard_map/ppermute | solution.py:19
  233.5 2.8 copy-start.1
  238.8 2.7 copy-start.2
  260.0 2.4 copy-start.7
  262.4 1.5 copy-start.5
  265.4 2.4 copy-start.3
where the time goes:
time: 325 us; the launch traced here: 322 us
  waiting for transfers between devices  136 us (42%)
  starting transfers between devices  83.1 us (26%)
  blocking collectives  45.8 us (14%)
  matrix products  33.4 us (10%)
  other arithmetic  15.7 us (5%)
  local copies, waits for them, and re-layouts  7.92 us (2%)
    ppermute x8, waiting for transfers between devices, passed_along(): lax.ppermute(value, axis, [(source, source + steps) for source in range(l...  132 us
    ppermute x8, starting transfers between devices, passed_along(): lax.ppermute(value, axis, [(source, source + steps) for source in range(l...  63.9 us
    all_to_all x1, blocking collectives, per_device(): lax.all_to_all(ordered, 'ctx', split_axis=0, concat_axis=0, tiled=True)  45.8 us
    dot_general x9, matrix products, update(): jnp.einsum('qgjk,kgd->qgjd', weights.astype(jnp.bfloat16), shard_values,...  20.7 us
    dot_general x9, matrix products, update(): jnp.einsum('qgjd,kgd->qgjk', query_block, shard_keys, preferred_element_t...  12.6 us
    all_to_all x1, starting transfers between devices, per_device(): lax.all_to_all(keys, 'head', split_axis=1, concat_axis=0, tiled=True)  10.1 us
    reduce_sum x9, other arithmetic, update(): new_total = old_total * factor + jnp.sum(weights, axis=-1)  9.67 us
  transfers between devices with their start and end apart: 11, of which 5 were waited for; matrix products, arithmetic and copies ran while one was open for 7% of the time, Pallas kernels for 0%

commit v1 on v0

v1 whole, which is shorter than its diff:
```python
import math

import jax
import jax.numpy as jnp
from jax import lax
from jax.experimental import pallas as pl
from jax.experimental.pallas import tpu as pltpu
from jax.sharding import PartitionSpec as P

HD = 128
QPK = 4
MOST = 4096
NDOC = 16
Y = 4
Z = 16
CTX = Y * Z
HEADS = 8
TOK = 512
OWN = TOK // HEADS
REACH = MOST // TOK
PIECE = TOK // CTX
ROWS = 256
CHUNKS = 4
HALF = TOK // 2
MESH = pl.DeviceIdType.MESH
masked_score = -1e30
FACTOR = math.log2(math.e) / math.sqrt(HD)


def wide(x, n):
    return jnp.concatenate([x] * n, axis=1)


def kernel(
    q_ref,
    k_ref,
    v_ref,
    docs,
    owner,
    out,
    qbuf,
    kv,
    first,
    top,
    acc,
    att,
    ordered,
    q_send,
    q_recv,
    kv_send,
    kv_recv,
    ring_send,
    ring_recv,
    out_send,
    out_recv,
    local,
):
    ctx = lax.axis_index("ctx")
    head = lax.axis_index("head")
    cy, cz = ctx // Z, ctx % Z

    def target_of(o):
        dy = 3 - o % Y
        k = o // Y
        size = 8 - (k + 1) // 2
        dz = jnp.where(k % 2 == 1, size, Z - size)
        return ((cy + dy) % Y) * Z + (cz + dz) % Z

    barrier = pltpu.get_barrier_semaphore()
    for o in range(1, HEADS):
        pl.semaphore_signal(
            barrier, inc=1, device_id=(ctx, (head + o) % HEADS), device_id_type=MESH
        )

    def greet(o, c):
        pl.semaphore_signal(barrier, inc=1, device_id=(target_of(o), head), device_id_type=MESH)
        return c

    lax.fori_loop(0, CTX - 1, greet, 0)
    pl.semaphore_wait(barrier, HEADS - 1 + CTX - 1)

    def cols(h, n):
        return pl.ds(pl.multiple_of(h * n, n), n)

    def rows_of(h):
        return pl.ds(pl.multiple_of(h * OWN, OWN), OWN)

    sides = (k_ref, v_ref)

    def kv_copy(o, side, source, target):
        return pltpu.make_async_remote_copy(
            src_ref=sides[side].at[:, cols(target, HD)],
            dst_ref=kv.at[0, side, rows_of(source)],
            send_sem=kv_send.at[o, side],
            recv_sem=kv_recv.at[o, side],
            device_id=(ctx, target),
            device_id_type=MESH,
        )

    def q_copy(o, source, target):
        return pltpu.make_async_remote_copy(
            src_ref=q_ref.at[:, cols(target, QPK * HD)],
            dst_ref=qbuf.at[rows_of(source)],
            send_sem=q_send.at[o],
            recv_sem=q_recv.at[o],
            device_id=(ctx, target),
            device_id_type=MESH,
        )

    for side in range(2):
        for o in range(1, HEADS):
            kv_copy(o, side, head, (head + o) % HEADS).start()
    for o in range(1, HEADS):
        q_copy(o, head, (head + o) % HEADS).start()
    own = [
        pltpu.make_async_copy(
            sides[side].at[:, cols(head, HD)], kv.at[0, side, rows_of(head)], local.at[side]
        )
        for side in range(2)
    ]
    own.append(
        pltpu.make_async_copy(
            q_ref.at[:, cols(head, QPK * HD)], qbuf.at[rows_of(head)], local.at[2]
        )
    )
    for copy in own:
        copy.start()

    following = (ctx + 1) % CTX

    def ring_copy(d, chunk):
        side, part = chunk // 2, chunk % 2
        return pltpu.make_async_remote_copy(
            src_ref=kv.at[d - 1, side, pl.ds(part * HALF, HALF)],
            dst_ref=kv.at[d, side, pl.ds(part * HALF, HALF)],
            send_sem=ring_send.at[d - 1, chunk],
            recv_sem=ring_recv.at[d - 1, chunk],
            device_id=(following, head),
            device_id_type=MESH,
        )

    for side in range(2):
        own[side].wait()
        for o in range(1, HEADS):
            kv_copy(o, side, (head - o) % HEADS, head).wait_recv()
        for part in range(2):
            ring_copy(1, side * 2 + part).start()

    place = ctx * TOK + lax.broadcasted_iota(jnp.int32, (TOK, HD), 0)
    begin = jnp.zeros((TOK, HD), jnp.int32)
    end = jnp.int32(0)
    for i in range(NDOC):
        end = end + docs[i]
        begin = jnp.where(place >= end, end, begin)
    first[...] = begin

    own[2].wait()
    for o in range(1, HEADS):
        q_copy(o, (head - o) % HEADS, head).wait_recv()

    def attend(d, diagonal):
        tiles = TOK // ROWS
        k_block = kv[d, 0]
        v_block = jnp.concatenate([kv[d, 1], jnp.ones((TOK, HD), jnp.bfloat16)], axis=1)
        base = (ctx - d) * TOK
        column = lax.broadcasted_iota(jnp.int32, (ROWS, TOK), 1)
        for j in range(QPK):

            def one(t, c):
                rows = pl.ds(pl.multiple_of(t * ROWS, ROWS), ROWS)
                q = qbuf[rows, j * HD : (j + 1) * HD]
                s = lax.dot_general(
                    q, k_block, (((1,), (1,)), ((), ())), preferred_element_type=jnp.float32
                )
                live = column >= wide(first[rows] - base, TOK // HD)
                if diagonal:
                    row = t * ROWS + lax.broadcasted_iota(jnp.int32, (ROWS, TOK), 0)
                    live = live & (column <= row)
                s = jnp.where(live, s, masked_score)
                peak = jnp.broadcast_to(jnp.max(s, axis=1, keepdims=True), (ROWS, HD))
                if diagonal:
                    new = peak
                else:
                    old = top[j, rows]
                    new = jnp.maximum(old, peak)
                p = jnp.exp2((s - wide(new, TOK // HD)) * FACTOR).astype(jnp.bfloat16)
                pv = jnp.dot(p, v_block, preferred_element_type=jnp.float32)
                if not diagonal:
                    keep = jnp.exp2((old - new) * FACTOR)
                    pv = pv + acc[j, rows] * wide(keep, 2)
                acc[j, rows] = pv
                top[j, rows] = new
                return c

            lax.fori_loop(0, tiles, one, 0)

    attend(0, True)

    def step(d, c):
        for chunk in range(CHUNKS):
            ring_copy(d, chunk).wait_recv()

            @pl.when(d < REACH)
            def _():
                ring_copy(d + 1, chunk).start()

        attend(d, False)
        return c

    lax.fori_loop(1, REACH + 1, step, 0)

    for j in range(QPK):
        att[:, j * HD : (j + 1) * HD] = (acc[j, :, :HD] / acc[j, :, HD:]).astype(jnp.bfloat16)
    spread = (
        lax.broadcasted_iota(jnp.int32, (CTX, TOK), 1) // PIECE
        == lax.broadcasted_iota(jnp.int32, (CTX, TOK), 0)
    ).astype(jnp.bfloat16)
    owners = jnp.broadcast_to(owner[...].astype(jnp.float32), (8, CTX)).astype(jnp.bfloat16)
    owner_of = jnp.dot(owners, spread, preferred_element_type=jnp.float32).astype(jnp.int32)
    column = lax.broadcasted_iota(jnp.int32, (8, TOK), 1)
    goal = (owner_of * PIECE + column % PIECE)[:1]
    swap = (lax.broadcasted_iota(jnp.int32, (TOK, TOK), 0) == goal).astype(jnp.bfloat16)
    moved = jnp.dot(swap, att[...], preferred_element_type=jnp.float32)
    ordered[...] = moved.reshape(CTX, PIECE, QPK * HD).astype(jnp.bfloat16)

    def deliver(o, c):
        target = target_of(o)
        pltpu.make_async_remote_copy(
            src_ref=ordered.at[target],
            dst_ref=out.at[ctx],
            send_sem=out_send,
            recv_sem=out_recv,
            device_id=(target, head),
            device_id_type=MESH,
        ).start()
        return c

    lax.fori_loop(0, CTX - 1, deliver, 0)
    mine = pltpu.make_async_copy(ordered.at[ctx], out.at[ctx], local.at[3])
    mine.start()

    for side in range(2):
        for o in range(1, HEADS):
            kv_copy(o, side, head, (head + o) % HEADS).wait_send()
    for o in range(1, HEADS):
        q_copy(o, head, (head + o) % HEADS).wait_send()

    def drain(d, c):
        for chunk in range(CHUNKS):
            ring_copy(d, chunk).wait_send()
        return c

    lax.fori_loop(1, REACH + 1, drain, 0)
    mine.wait()
    rest = pltpu.make_async_remote_copy(
        src_ref=ordered.at[pl.ds(0, CTX - 1)],
        dst_ref=out.at[pl.ds(0, CTX - 1)],
        send_sem=out_send,
        recv_sem=out_recv,
        device_id=(following, head),
        device_id_type=MESH,
    )
    rest.wait_send()
    rest.wait_recv()


def per_device(queries, keys, values, doc_lengths, piece_owner):
    whole = pl.BlockSpec(memory_space=pl.ANY)
    owned = pl.pallas_call(
        kernel,
        out_shape=jax.ShapeDtypeStruct((CTX, PIECE, QPK * HD), jnp.bfloat16),
        in_specs=[
            whole,
            whole,
            whole,
            pl.BlockSpec(memory_space=pltpu.SMEM),
            pl.BlockSpec(memory_space=pltpu.VMEM),
        ],
        out_specs=whole,
        scratch_shapes=[
            pltpu.VMEM((TOK, QPK * HD), jnp.bfloat16),
            pltpu.VMEM((REACH + 1, 2, TOK, HD), jnp.bfloat16),
            pltpu.VMEM((TOK, HD), jnp.int32),
            pltpu.VMEM((QPK, TOK, HD), jnp.float32),
            pltpu.VMEM((QPK, TOK, 2 * HD), jnp.float32),
            pltpu.VMEM((TOK, QPK * HD), jnp.bfloat16),
            pltpu.VMEM((CTX, PIECE, QPK * HD), jnp.bfloat16),
            pltpu.SemaphoreType.DMA((HEADS,)),
            pltpu.SemaphoreType.DMA((HEADS,)),
            pltpu.SemaphoreType.DMA((HEADS, 2)),
            pltpu.SemaphoreType.DMA((HEADS, 2)),
            pltpu.SemaphoreType.DMA((REACH, CHUNKS)),
            pltpu.SemaphoreType.DMA((REACH, CHUNKS)),
            pltpu.SemaphoreType.DMA,
            pltpu.SemaphoreType.DMA,
            pltpu.SemaphoreType.DMA((4,)),
        ],
        compiler_params=pltpu.CompilerParams(
            collective_id=0, has_side_effects=True, vmem_limit_bytes=32 * 1024 * 1024
        ),
    )(queries, keys, values, doc_lengths, piece_owner)
    return owned.reshape(TOK, QPK * HD)


def solution(mesh):
    return jax.shard_map(
        per_device,
        mesh=mesh,
        in_specs=(
            P(("ctx", "head"), None),
            P(("ctx", "head"), None),
            P(("ctx", "head"), None),
            P(),
            P("ctx", None),
        ),
        out_specs=P("ctx", "head"),
        check_vma=False,
    )
```

time: 325 us -> 111 us (0.34)
  waiting for transfers between devices: 136 us -> 0 us
  Pallas kernels: 0 us -> 106 us
  starting transfers between devices: 83.1 us -> 0 us
  blocking collectives: 45.8 us -> 0 us
  matrix products: 33.4 us -> 0 us
  other arithmetic: 15.7 us -> 0 us
    ppermute x8 -> x0, waiting for transfers between devices: 132 us -> none  [passed_along(): lax.ppermute(value, axis, [(source, source + steps) for source in range(l...]
    pallas_call x0 -> x1, Pallas kernels: none -> 106 us  [per_device(): pl.pallas_call(kernel, out_shape=jax.ShapeDtypeStruct((CTX, PIECE, QPK *...]
    ppermute x8 -> x0, starting transfers between devices: 63.9 us -> none  [passed_along(): lax.ppermute(value, axis, [(source, source + steps) for source in range(l...]
    all_to_all x1 -> x0, blocking collectives: 45.8 us -> none  [per_device(): lax.all_to_all(ordered, 'ctx', split_axis=0, concat_axis=0, tiled=True)]
    dot_general x18 -> x0, matrix products: 33.4 us -> none  [the longest x9 20.7 us: update(): jnp.einsum('qgjk,kgd->qgjd', weights.astype(jnp.bfloat16), shard_values,...]
    all_to_all x3 -> x0, starting transfers between devices: 19.2 us -> none  [the longest x1 10.1 us: per_device(): lax.all_to_all(keys, 'head', split_axis=1, concat_axis=0, tiled=True)]
    reduce_sum x11 -> x0, other arithmetic: 10.6 us -> none  [the longest x9 9.67 us: update(): new_total = old_total * factor + jnp.sum(weights, axis=-1)]
    all_to_all x3 -> x0, local copies, waits for them, and re-layouts: 4.13 us -> none  [the longest x1 1.89 us: per_device(): lax.all_to_all(queries, 'head', split_axis=1, concat_axis=0, tiled=True)]
  transfers between devices with their start and end apart: 11 -> 0, of which waited for: 5 -> 0; matrix products, arithmetic and copies ran while one was open for 7% -> 0% of each run, Pallas kernels for 0% -> 0%
where the time goes in v1:
time: 111 us
  Pallas kernels  106 us (95%)
  local copies, waits for them, and re-layouts  4.95 us (4%)
    pallas_call x1, Pallas kernels, per_device(): pl.pallas_call(kernel, out_shape=jax.ShapeDtypeStruct((CTX, PIECE, QPK *...  106 us
    unnamed x11, local copies, waits for them, and re-layouts  4.95 us

profile of v1, /device:TPU:1, one launch (start us, length us, event | category | flops | bytes accessed | tf_op | source)
XLA Modules:
  0.0 111.0 jit_solution(11122580904934269541)
XLA Ops:
  0.0 0.0 copy-start
  0.0 1.0 copy-done
  1.0 0.0 copy-start.1
  1.0 0.9 copy-done.1
  1.9 0.0 copy-start.2
  1.9 0.9 copy-done.2
  2.9 0.0 copy-start.3
  2.9 0.7 copy-done.3
  3.5 0.0 copy-start.4
  3.5 0.7 copy-done.4
  4.2 106.0 %shard_map.55 = bf16[64,8,512]{2,1,0:T(8,128)(2,1)S(1)} custom-call(bf16[64,4096]{1,0:T(8,128)(2,1)S(1)} %copy-done, bf16[64,1024]{1,0:T(8,128)(2,1)S(1)} %copy-done.1, bf16[64,1024]{1,0:T(8,128)(2,1)S(1)} %copy-done.2, s32[16]{0:T(128)S(1)} %copy-done.3, s32[1,64]{1,0:T(1,128)S(1)} %copy-done.4), custom_call_target="tpu_custom_call" | custom-call | tf_op jit(solution)/shard_map/pallas_call | solution.py:269
  110.2 0.8 copy.7
Async XLA Ops:
  0.0 1.0 copy-start
  1.0 0.9 copy-start.1
  1.9 0.9 copy-start.2
  2.9 0.7 copy-start.3
  3.5 0.7 copy-start.4

commit v2 on v1

v2 whole, which is shorter than its diff:
```python
import math

import jax
import jax.numpy as jnp
from jax import lax
from jax.experimental import pallas as pl
from jax.experimental.pallas import tpu as pltpu
from jax.sharding import PartitionSpec as P

HD = 128
QPK = 4
MOST = 4096
NDOC = 16
Y = 4
Z = 16
CTX = Y * Z
HEADS = 8
TOK = 512
OWN = TOK // HEADS
REACH = MOST // TOK
PIECE = TOK // CTX
ROWS = 256
EXTRA = 16
WIDE = 256
CHUNK = 64
CHUNKS = TOK // CHUNK
MESH = pl.DeviceIdType.MESH
dead_score = -1e30
FACTOR = math.log2(math.e) / math.sqrt(HD)


def kernel(
    q_ref,
    k_ref,
    v_ref,
    docs_ref,
    owner_ref,
    out,
    docs,
    owner,
    qbuf,
    kv,
    qdoc,
    qt,
    kdoc,
    top,
    acc,
    att,
    swap,
    ordered,
    q_send,
    q_recv,
    kv_send,
    kv_recv,
    ring_send,
    ring_recv,
    out_send,
    out_recv,
    local,
    from_left,
    from_right,
):
    ctx = lax.axis_index("ctx")
    head = lax.axis_index("head")
    cy, cz = lax.div(ctx, Z), lax.rem(ctx, Z)

    def at(dy, dz):
        return lax.rem(cy + dy, Y) * Z + lax.rem(cz + dz, Z)

    tables = [
        pltpu.make_async_copy(docs_ref, docs, local.at[4]),
        pltpu.make_async_copy(owner_ref, owner, local.at[5]),
    ]
    for copy in tables:
        copy.start()
    following, previous = lax.rem(ctx + 1, CTX), lax.rem(ctx + CTX - 1, CTX)
    left, right = at(0, Z - 1), at(0, 1)
    barrier = pltpu.get_barrier_semaphore()

    def signal(sem, where):
        pl.semaphore_signal(sem, inc=1, device_id=where, device_id_type=MESH)

    for o in range(1, HEADS):
        signal(barrier, (ctx, lax.rem(head + o, HEADS)))
    near = (following, previous, left, right, at(1, 0), at(2, 0), at(3, 0))
    for place in near:
        signal(barrier, (place, head))
    pl.semaphore_wait(barrier, HEADS - 1 + len(near))

    def cols(h, n):
        return pl.ds(pl.multiple_of(h * n, n), n)

    def rows_of(h):
        return pl.ds(pl.multiple_of(h * OWN, OWN), OWN)

    sides = (k_ref, v_ref)

    def kv_copy(o, side, source, target):
        return pltpu.make_async_remote_copy(
            src_ref=sides[side].at[:, cols(target, HD)],
            dst_ref=kv.at[0, side, rows_of(source)],
            send_sem=kv_send.at[o, side],
            recv_sem=kv_recv.at[o, side],
            device_id=(ctx, target),
            device_id_type=MESH,
        )

    def q_copy(o, source, target):
        return pltpu.make_async_remote_copy(
            src_ref=q_ref.at[:, cols(target, QPK * HD)],
            dst_ref=qbuf.at[rows_of(source)],
            send_sem=q_send.at[o],
            recv_sem=q_recv.at[o],
            device_id=(ctx, target),
            device_id_type=MESH,
        )

    def peer(o):
        return lax.rem(head + o, HEADS)

    def source(o):
        return lax.rem(head + HEADS - o, HEADS)

    for side in range(2):
        for o in range(1, HEADS):
            kv_copy(o, side, head, peer(o)).start()
    for o in range(1, HEADS):
        q_copy(o, head, peer(o)).start()
    own = [
        pltpu.make_async_copy(
            sides[side].at[:, cols(head, HD)], kv.at[0, side, rows_of(head)], local.at[side]
        )
        for side in range(2)
    ]
    own.append(
        pltpu.make_async_copy(
            q_ref.at[:, cols(head, QPK * HD)], qbuf.at[rows_of(head)], local.at[2]
        )
    )
    for copy in own:
        copy.start()

    def greet():
        signal(from_left, (right, head))
        signal(from_right, (left, head))
        pl.semaphore_wait(from_left, 1)
        pl.semaphore_wait(from_right, 1)

    def ring_copy(n):
        d, begin = lax.div(n, CHUNKS), pl.multiple_of(lax.rem(n, CHUNKS) * CHUNK, CHUNK)
        return pltpu.make_async_remote_copy(
            src_ref=kv.at[d, :, pl.ds(begin, CHUNK)],
            dst_ref=kv.at[d + 1, :, pl.ds(begin, CHUNK)],
            send_sem=ring_send.at[n],
            recv_sem=ring_recv.at[n],
            device_id=(following, head),
            device_id_type=MESH,
        )

    for side in range(2):
        own[side].wait()
        for o in range(1, HEADS):
            kv_copy(o, side, source(o), head).wait_recv()
    for n in range(CHUNKS):
        ring_copy(n).start()

    for copy in tables:
        copy.wait()
    lane = lax.broadcasted_iota(jnp.int32, (TOK, HD), 1)
    row = lax.broadcasted_iota(jnp.int32, (TOK, HD), 0)
    low = jnp.full((TOK, HD), CTX * TOK, jnp.int32)
    high = jnp.zeros((TOK, HD), jnp.int32)
    end = jnp.int32(0)
    for i in range(NDOC):
        low = jnp.where(lane == i, end, low)
        end = end + docs[i]
        high = jnp.where(lane == i, end, high)

    def member(d):
        place = lax.rem(ctx + CTX - d, CTX) * TOK + row
        return (place >= low) & (place < high)

    qdoc[...] = jnp.where(member(0), 1.0, 0.0).astype(jnp.bfloat16)

    def mark(d, c):
        kdoc[d] = jnp.where(member(d), 0.0, dead_score).astype(jnp.bfloat16)
        return c

    lax.fori_loop(0, REACH + 1, mark, 0)

    spread = (
        lax.div(lax.broadcasted_iota(jnp.int32, (CTX, TOK), 1), PIECE)
        == lax.broadcasted_iota(jnp.int32, (CTX, TOK), 0)
    ).astype(jnp.bfloat16)
    owners = jnp.broadcast_to(owner[...].astype(jnp.float32), (8, CTX)).astype(jnp.bfloat16)
    owner_of = jnp.dot(owners, spread, preferred_element_type=jnp.float32).astype(jnp.int32)
    column = lax.broadcasted_iota(jnp.int32, (8, TOK), 1)
    goal = (owner_of * PIECE + lax.rem(column, PIECE))[:1]
    swap[...] = (lax.broadcasted_iota(jnp.int32, (TOK, TOK), 0) == goal).astype(jnp.bfloat16)

    own[2].wait()
    for o in range(1, HEADS):
        q_copy(o, source(o), head).wait_recv()

    eye = (
        lax.broadcasted_iota(jnp.int32, (HD, HD), 0) == lax.broadcasted_iota(jnp.int32, (HD, HD), 1)
    ).astype(jnp.bfloat16)
    ones = jnp.ones((EXTRA, WIDE), jnp.bfloat16)

    def across(a, b):
        return lax.dot_general(a, b, (((1,), (1,)), ((), ())), preferred_element_type=jnp.float32)

    for j in range(QPK):
        qt[j, :HD] = across(eye, qbuf[:, j * HD : (j + 1) * HD]).astype(jnp.bfloat16)
        qt[j, HD:] = across(eye, qdoc[...]).astype(jnp.bfloat16)

    def attend(k_rows, k_docs, v_rows, tiles=range(TOK // ROWS), causal=False, fresh=False):
        k_all = jnp.concatenate([k_rows, k_docs], axis=1)
        v_all = jnp.concatenate([across(eye, v_rows).astype(jnp.bfloat16), ones], axis=0)

        def score(j, t):
            rows = slice(t * ROWS, (t + 1) * ROWS)
            s = jnp.dot(k_all, qt[j, :, rows], preferred_element_type=jnp.float32)
            if causal:
                key = lax.broadcasted_iota(jnp.int32, (WIDE, ROWS), 0)
                query = lax.broadcasted_iota(jnp.int32, (WIDE, ROWS), 1)
                s = jnp.where(key <= query, s, dead_score)
            return s

        def weigh(j, t, s):
            rows = slice(t * ROWS, (t + 1) * ROWS)
            peak = jnp.max(s, axis=0, keepdims=True)
            if fresh:
                new, keep = peak, None
            else:
                old = top[j, :1, rows]
                new = jnp.maximum(old, peak)
                keep = jnp.exp2((old - new) * FACTOR)
            top[j, :1, rows] = new
            return jnp.exp2((s - new) * FACTOR).astype(jnp.bfloat16), keep

        def gather(j, t, p, keep):
            rows = slice(t * ROWS, (t + 1) * ROWS)
            pv = jnp.dot(v_all, p, preferred_element_type=jnp.float32)
            if keep is not None:
                pv = pv + acc[j, :, rows] * keep
            acc[j, :, rows] = pv

        order = [(j, t) for j in range(QPK) for t in tiles]
        ss = {0: score(*order[0])}
        pp = {}
        for i in range(len(order) + 1):
            if i + 1 < len(order):
                ss[i + 1] = score(*order[i + 1])
            if i > 0:
                gather(*order[i - 1], *pp[i - 1])
            if i < len(order):
                pp[i] = weigh(*order[i], ss[i])

    def block(begin):
        rows = slice(begin, begin + WIDE)
        return kv[0, 0, rows], kdoc[0, rows], kv[0, 1, rows]

    attend(*block(0), tiles=(0,), causal=True, fresh=True)
    attend(*block(0), tiles=(1,), fresh=True)
    attend(*block(WIDE), tiles=(1,), causal=True)

    def arrive(u):
        for i in range(CHUNKS // 2):
            n = u * (CHUNKS // 2) + i
            ring_copy(n).wait_recv()

            @pl.when(n < (REACH - 1) * CHUNKS)
            def _():
                ring_copy(n + CHUNKS).start()

    def unit(u):
        d = lax.div(u, 2) + 1
        rows = pl.ds(pl.multiple_of(lax.rem(u, 2) * WIDE, WIDE), WIDE)
        attend(kv[d, 0, rows], kdoc[d, rows], kv[d, 1, rows])

    arrive(0)

    def step(u, c):
        arrive(u)
        pl.when(u <= Z // 2)(greet)
        unit(u - 1)
        return c

    lax.fori_loop(1, 2 * REACH, step, 0)
    unit(2 * REACH - 1)

    for j in range(QPK):
        att[j * HD : (j + 1) * HD] = (acc[j, :HD] / acc[j, HD : HD + 1]).astype(jnp.bfloat16)
    ordered[...] = (
        across(swap[...], att[...]).reshape(CTX, PIECE, QPK * HD).astype(jnp.bfloat16)
    )

    def deliver(o, c):
        k = lax.div(o, Y)
        size = Z // 2 - lax.div(k + 1, 2)
        dz = jnp.where(lax.rem(k, 2) == 1, size, Z - size)
        target = at(Y - 1 - lax.rem(o, Y), dz)
        pltpu.make_async_remote_copy(
            src_ref=ordered.at[target],
            dst_ref=out.at[ctx],
            send_sem=out_send,
            recv_sem=out_recv,
            device_id=(target, head),
            device_id_type=MESH,
        ).start()
        return c

    lax.fori_loop(0, CTX - 1, deliver, 0)
    mine = pltpu.make_async_copy(ordered.at[ctx], out.at[ctx], local.at[3])
    mine.start()

    for side in range(2):
        for o in range(1, HEADS):
            kv_copy(o, side, head, peer(o)).wait_send()
    for o in range(1, HEADS):
        q_copy(o, head, peer(o)).wait_send()

    def drain(n, c):
        ring_copy(n).wait_send()
        return c

    lax.fori_loop(0, REACH * CHUNKS, drain, 0)
    mine.wait()
    rest = pltpu.make_async_remote_copy(
        src_ref=ordered.at[pl.ds(0, CTX - 1)],
        dst_ref=out.at[pl.ds(0, CTX - 1)],
        send_sem=out_send,
        recv_sem=out_recv,
        device_id=(following, head),
        device_id_type=MESH,
    )
    rest.wait_send()
    rest.wait_recv()


def per_device(queries, keys, values, doc_lengths, piece_owner):
    whole = pl.BlockSpec(memory_space=pltpu.HBM)
    dma = pltpu.SemaphoreType.DMA
    owned = pl.pallas_call(
        kernel,
        out_shape=jax.ShapeDtypeStruct((CTX, PIECE, QPK * HD), jnp.bfloat16),
        in_specs=[
            whole,
            whole,
            whole,
            whole,
            whole,
        ],
        out_specs=pl.BlockSpec(memory_space=pl.ANY),
        scratch_shapes=[
            pltpu.SMEM((NDOC,), jnp.int32),
            pltpu.VMEM((1, CTX), jnp.int32),
            pltpu.VMEM((TOK, QPK * HD), jnp.bfloat16),
            pltpu.VMEM((REACH + 1, 2, TOK, HD), jnp.bfloat16),
            pltpu.VMEM((TOK, HD), jnp.bfloat16),
            pltpu.VMEM((QPK, 2 * HD, TOK), jnp.bfloat16),
            pltpu.VMEM((REACH + 1, TOK, HD), jnp.bfloat16),
            pltpu.VMEM((QPK, 8, TOK), jnp.float32),
            pltpu.VMEM((QPK, HD + EXTRA, TOK), jnp.float32),
            pltpu.VMEM((QPK * HD, TOK), jnp.bfloat16),
            pltpu.VMEM((TOK, TOK), jnp.bfloat16),
            pltpu.VMEM((CTX, PIECE, QPK * HD), jnp.bfloat16),
            dma((HEADS,)),
            dma((HEADS,)),
            dma((HEADS, 2)),
            dma((HEADS, 2)),
            dma((REACH * CHUNKS,)),
            dma((REACH * CHUNKS,)),
            dma,
            dma,
            dma((6,)),
            pltpu.SemaphoreType.REGULAR,
            pltpu.SemaphoreType.REGULAR,
        ],
        compiler_params=pltpu.CompilerParams(
            collective_id=0, has_side_effects=True, vmem_limit_bytes=66_000_000
        ),
    )(queries, keys, values, doc_lengths, piece_owner)
    return owned.reshape(TOK, QPK * HD)


def solution(mesh):
    return jax.shard_map(
        per_device,
        mesh=mesh,
        in_specs=(
            P(("ctx", "head"), None),
            P(("ctx", "head"), None),
            P(("ctx", "head"), None),
            P(),
            P("ctx", None),
        ),
        out_specs=P("ctx", "head"),
        check_vma=False,
    )
```

time: 111 us -> 100 us (0.901)
  Pallas kernels: 106 us -> 97.9 us
  local copies, waits for them, and re-layouts: 4.95 us -> 1.87 us
    pallas_call x1, Pallas kernels: 106 us -> 97.9 us  [per_device(): pl.pallas_call(kernel, out_shape=jax.ShapeDtypeStruct((CTX, PIECE, QPK *...]
    unnamed x11 -> x1, local copies, waits for them, and re-layouts: 4.95 us -> 1.87 us
where the time goes in v2:
time: 100 us; the launch traced here: 99.8 us
  Pallas kernels  97.9 us (98%)
  local copies, waits for them, and re-layouts  1.87 us (2%)
    pallas_call x1, Pallas kernels, per_device(): pl.pallas_call(kernel, out_shape=jax.ShapeDtypeStruct((CTX, PIECE, QPK *...  97.9 us

profile of v2, /device:TPU:1, one launch (start us, length us, event | category | flops | bytes accessed | tf_op | source)
XLA Modules:
  0.0 99.8 jit_solution(16969870716586220377)
XLA Ops:
  0.0 97.9 %shard_map.55 = bf16[64,8,512]{2,1,0:T(8,128)(2,1)} custom-call(bf16[64,4096]{1,0:T(8,128)(2,1)} %q_ref.1, bf16[64,1024]{1,0:T(8,128)(2,1)} %k_ref.1, bf16[64,1024]{1,0:T(8,128)(2,1)} %v_ref.1, s32[16]{0:T(128)} %docs_ref.1, s32[1,64]{1,0:T(1,128)} %owner_ref.1), custom_call_target="tpu_custom_call" | custom-call | tf_op jit(solution)/shard_map/pallas_call | solution.py:345
  98.0 1.9 %copy.7 = bf16[512,512]{1,0:T(8,128)(2,1)} copy(bf16[512,512]{1,0:T(8,128)(2,1)} %bitcast.1) | data formatting | bytes 1048576

commit v3 on v2

--- a/solution.py
+++ b/solution.py
@@ -15,6 +15,7 @@
 Z = 16
 CTX = Y * Z
 HEADS = 8
+HALF = HEADS // 2
 TOK = 512
 OWN = TOK // HEADS
 REACH = MOST // TOK
@@ -22,8 +23,6 @@
 ROWS = 256
 EXTRA = 16
 WIDE = 256
-CHUNK = 64
-CHUNKS = TOK // CHUNK
 MESH = pl.DeviceIdType.MESH
 dead_score = -1e30
 FACTOR = math.log2(math.e) / math.sqrt(HD)
@@ -115,14 +114,20 @@
             device_id_type=MESH,
         )
 
-    def peer(o):
-        return lax.rem(head + o, HEADS)
-
-    def source(o):
-        return lax.rem(head + HEADS - o, HEADS)
-
-    for side in range(2):
-        for o in range(1, HEADS):
+    half, place_in = lax.div(head, HALF), lax.rem(head, HALF)
+
+    def other(i, step):
+        side = half if i < HALF else 1 - half
+        return side * HALF + lax.rem(place_in + HALF + step * (i % HALF), HALF)
+
+    def peer(i):
+        return other(i, 1)
+
+    def source(i):
+        return other(i, -1)
+
+    for o in range(1, HEADS):
+        for side in range(2):
             kv_copy(o, side, head, peer(o)).start()
     for o in range(1, HEADS):
         q_copy(o, head, peer(o)).start()
@@ -146,23 +151,33 @@
         pl.semaphore_wait(from_left, 1)
         pl.semaphore_wait(from_right, 1)
 
-    def ring_copy(n):
-        d, begin = lax.div(n, CHUNKS), pl.multiple_of(lax.rem(n, CHUNKS) * CHUNK, CHUNK)
+    def ring_copy(d, i):
+        rows = rows_of(source(i))
         return pltpu.make_async_remote_copy(
-            src_ref=kv.at[d, :, pl.ds(begin, CHUNK)],
-            dst_ref=kv.at[d + 1, :, pl.ds(begin, CHUNK)],
-            send_sem=ring_send.at[n],
-            recv_sem=ring_recv.at[n],
+            src_ref=kv.at[d - 1, :, rows],
+            dst_ref=kv.at[d, :, rows],
+            send_sem=ring_send.at[d - 1, i],
+            recv_sem=ring_recv.at[d - 1, i],
             device_id=(following, head),
             device_id_type=MESH,
         )
 
-    for side in range(2):
-        own[side].wait()
-        for o in range(1, HEADS):
-            kv_copy(o, side, source(o), head).wait_recv()
-    for n in range(CHUNKS):
-        ring_copy(n).start()
+    for i in range(HEADS):
+        for side in range(2):
+            if i == 0:
+                own[side].wait()
+            else:
+                kv_copy(i, side, source(i), head).wait_recv()
+        ring_copy(1, i).start()
+
+    def arrive(u):
+        d = lax.div(u, 2) + 1
+        for i in range(HEADS):
+
+            @pl.when(lax.rem(u, 2) == i // HALF)
+            def _():
+                ring_copy(d, i).wait_recv()
+                pl.when(d < REACH)(ring_copy(d + 1, i).start)
 
     for copy in tables:
         copy.wait()
@@ -198,6 +213,8 @@
     goal = (owner_of * PIECE + lax.rem(column, PIECE))[:1]
     swap[...] = (lax.broadcasted_iota(jnp.int32, (TOK, TOK), 0) == goal).astype(jnp.bfloat16)
 
+    for u in range(3):
+        arrive(jnp.int32(u))
     own[2].wait()
     for o in range(1, HEADS):
         q_copy(o, source(o), head).wait_recv()
@@ -265,30 +282,25 @@
     attend(*block(0), tiles=(1,), fresh=True)
     attend(*block(WIDE), tiles=(1,), causal=True)
 
-    def arrive(u):
-        for i in range(CHUNKS // 2):
-            n = u * (CHUNKS // 2) + i
-            ring_copy(n).wait_recv()
-
-            @pl.when(n < (REACH - 1) * CHUNKS)
-            def _():
-                ring_copy(n + CHUNKS).start()
-
-    def unit(u):
+    def unit(u, c=0):
         d = lax.div(u, 2) + 1
-        rows = pl.ds(pl.multiple_of(lax.rem(u, 2) * WIDE, WIDE), WIDE)
+        side = jnp.where(lax.rem(u, 2) == 0, half, 1 - half)
+        rows = pl.ds(pl.multiple_of(side * WIDE, WIDE), WIDE)
         attend(kv[d, 0, rows], kdoc[d, rows], kv[d, 1, rows])
-
-    arrive(0)
+        return c
+
+    arrive(jnp.int32(3))
+    for u, units in ((4, (0, 2)), (5, (2, 4)), (6, (4, 5)), (7, (5, 7))):
+        arrive(jnp.int32(u))
+        lax.fori_loop(*units, unit, 0)
 
     def step(u, c):
         arrive(u)
-        pl.when(u <= Z // 2)(greet)
-        unit(u - 1)
-        return c
-
-    lax.fori_loop(1, 2 * REACH, step, 0)
-    unit(2 * REACH - 1)
+        greet()
+        return unit(u - 1, c)
+
+    lax.fori_loop(Z // 2, 2 * REACH, step, 0)
+    unit(jnp.int32(2 * REACH - 1))
 
     for j in range(QPK):
         att[j * HD : (j + 1) * HD] = (acc[j, :HD] / acc[j, HD : HD + 1]).astype(jnp.bfloat16)
@@ -321,11 +333,12 @@
     for o in range(1, HEADS):
         q_copy(o, head, peer(o)).wait_send()
 
-    def drain(n, c):
-        ring_copy(n).wait_send()
+    def drain(d, c):
+        for i in range(HEADS):
+            ring_copy(d, i).wait_send()
         return c
 
-    lax.fori_loop(0, REACH * CHUNKS, drain, 0)
+    lax.fori_loop(1, REACH + 1, drain, 0)
     mine.wait()
     rest = pltpu.make_async_remote_copy(
         src_ref=ordered.at[pl.ds(0, CTX - 1)],
@@ -370,8 +383,8 @@
             dma((HEADS,)),
             dma((HEADS, 2)),
             dma((HEADS, 2)),
-            dma((REACH * CHUNKS,)),
-            dma((REACH * CHUNKS,)),
+            dma((REACH, HEADS)),
+            dma((REACH, HEADS)),
             dma,
             dma,
             dma((6,)),

time: 100 us -> 97 us (0.970)
  Pallas kernels: 97.9 us -> 94.9 us
    pallas_call x1, Pallas kernels: 97.9 us -> 94.9 us  [per_device(): pl.pallas_call(kernel, out_shape=jax.ShapeDtypeStruct((CTX, PIECE, QPK *...]
where the time goes in v3:
time: 97 us; the launch traced here: 96.8 us
  Pallas kernels  94.9 us (98%)
  local copies, waits for them, and re-layouts  1.87 us (2%)
    pallas_call x1, Pallas kernels, per_device(): pl.pallas_call(kernel, out_shape=jax.ShapeDtypeStruct((CTX, PIECE, QPK *...  94.9 us

profile of v3, /device:TPU:1, one launch (start us, length us, event | category | flops | bytes accessed | tf_op | source)
XLA Modules:
  0.0 96.8 jit_solution(5273060940896596072)
XLA Ops:
  0.0 94.9 %shard_map.55 = bf16[64,8,512]{2,1,0:T(8,128)(2,1)} custom-call(bf16[64,4096]{1,0:T(8,128)(2,1)} %q_ref.1, bf16[64,1024]{1,0:T(8,128)(2,1)} %k_ref.1, bf16[64,1024]{1,0:T(8,128)(2,1)} %v_ref.1, s32[16]{0:T(128)} %docs_ref.1, s32[1,64]{1,0:T(1,128)} %owner_ref.1), custom_call_target="tpu_custom_call" | custom-call | tf_op jit(solution)/shard_map/pallas_call | solution.py:358
  95.0 1.9 %copy.7 = bf16[512,512]{1,0:T(8,128)(2,1)} copy(bf16[512,512]{1,0:T(8,128)(2,1)} %bitcast.1) | data formatting | bytes 1048576

commit v4 on v3

--- a/solution.py
+++ b/solution.py
@@ -309,10 +309,10 @@
     )
 
     def deliver(o, c):
-        k = lax.div(o, Y)
+        k = lax.rem(o, Z)
         size = Z // 2 - lax.div(k + 1, 2)
         dz = jnp.where(lax.rem(k, 2) == 1, size, Z - size)
-        target = at(Y - 1 - lax.rem(o, Y), dz)
+        target = at(Y - 1 - lax.div(o, Z), dz)
         pltpu.make_async_remote_copy(
             src_ref=ordered.at[target],
             dst_ref=out.at[ctx],

time: 97 us -> 96.5 us (level); the launches traced: 96.8 us -> 95 us
  Pallas kernels: 94.9 us -> 93.1 us
    pallas_call x1, Pallas kernels: 94.9 us -> 93.1 us  [per_device(): pl.pallas_call(kernel, out_shape=jax.ShapeDtypeStruct((CTX, PIECE, QPK *...]
where the time goes in v4:
time: 96.5 us; the launch traced here: 95 us
  Pallas kernels  93.1 us (96%)
  local copies, waits for them, and re-layouts  1.87 us (2%)
    pallas_call x1, Pallas kernels, per_device(): pl.pallas_call(kernel, out_shape=jax.ShapeDtypeStruct((CTX, PIECE, QPK *...  93.1 us

profile of v4, /device:TPU:1, one launch (start us, length us, event | category | flops | bytes accessed | tf_op | source)
XLA Modules:
  0.0 95.0 jit_solution(8605148749688836144)
XLA Ops:
  0.0 93.1 %shard_map.55 = bf16[64,8,512]{2,1,0:T(8,128)(2,1)} custom-call(bf16[64,4096]{1,0:T(8,128)(2,1)} %q_ref.1, bf16[64,1024]{1,0:T(8,128)(2,1)} %k_ref.1, bf16[64,1024]{1,0:T(8,128)(2,1)} %v_ref.1, s32[16]{0:T(128)} %docs_ref.1, s32[1,64]{1,0:T(1,128)} %owner_ref.1), custom_call_target="tpu_custom_call" | custom-call | tf_op jit(solution)/shard_map/pallas_call | solution.py:358
  93.1 1.9 %copy.7 = bf16[512,512]{1,0:T(8,128)(2,1)} copy(bf16[512,512]{1,0:T(8,128)(2,1)} %bitcast.1) | data formatting | bytes 1048576
